TPU v7x, 512 devices: a whole 4x8x8 slice. The times are simulated.
512 devices in a mesh: prow: 16 (over z_lo, x, core), pcol: 32 (over z_hi, y).
Axes of the slice: x: 4, y: 8, z: 8 (z_hi: 4, z_lo: 2; z = z_hi * 2 + z_lo), core: 2. Of those that a mesh axis runs over, the one named last changes fastest.
Arguments:
- trailing: float32 [8192, 8192], P('prow', 'pcol'), may hold values from -6 to 6
- panels: float32 [8192, 1024], P('prow', 'pcol'), may hold values from -0.09375 to 0.09375
- diag_inv: float32 [4, 256, 256], replicated, may hold values from -6 to 6
- ancestors: int32 [4, 16], replicated, may hold values from 0 to 31, as said below
- owner_map: int32 [32], replicated, may hold values from 0 to 31, each once
Outputs:
- inv_panel: float32 [8192, 1024], P(('prow', 'pcol'))
- inv_upper: float32 [1024, 8192], P('pcol', 'prow')
- inv_diag: float32 [4, 256, 256], replicated
Inputs may be any that keep to these rules, and one draw needn't show every extreme that they name: `ancestors`: each row names 16 distinct blocks; every block is named by exactly two siblings.
All inputs are finite; a program needn't handle non-finite values.
Results may differ from a plain program's by a relative error of at most 0.000071.
Values sent between devices are 32-bit elements; how exact they have to be, the bound alone decides.
No kernel may reach another device: no remote copies, remote signals or barrier semaphores. Data moves between devices by JAX's collectives and lax.ppermute only.
A program may use at most 64 MiB of HBM per device.

v0:
```python
import jax
import jax.numpy as jnp
from jax import lax
from jax.experimental import pallas as pl
from jax.experimental.pallas import tpu as pltpu
from jax.sharding import Mesh, PartitionSpec as P

NB = 256
SIBS = 4
CHIP = ("zlo", "xh", "xl")
PROW = CHIP + ("core",)
PCOL = ("zhi", "yhi", "ylo")
NROW = 16
CHIPS = 8
NCOL = 32
LANES = 128
HIGH = lax.Precision.HIGH


def exchange(array, axes):
    return lax.all_to_all(array, axes, 0, 0, tiled=True)


def to_all(array, count):
    return jnp.broadcast_to(array[None], (count,) + array.shape)


def column_of_block():
    pairs = []
    for p in range(NROW):
        for s in range(SIBS):
            for c in range(8):
                source = p * NCOL + s * 8 + c
                chip = c % 4 * 2 + s // 2
                target = (chip * 2 + c // 4) * NCOL + 2 * p + s % 2
                pairs.append((source, target))
    return pairs


def assemble_kernel(core_ref, mine_ref, other_ref, diag_ref, out_ref):
    low_is_mine = core_ref[0] == 0
    for a in range(2):
        for c in range(2):
            tiles = []
            for b in range(2):
                part = a * 4 + b * 2 + c
                mine, other = mine_ref[part], other_ref[part]
                tiles.append(
                    (
                        jnp.where(low_is_mine, mine, other),
                        jnp.where(low_is_mine, other, mine),
                    )
                )
            for e in range(2):
                rows = pl.ds((a * 4 + e * 2 + c) * 32, 32)
                for half in range(2):
                    term = jnp.concatenate(
                        [tiles[b][half][:, e * 64 : e * 64 + 64] for b in range(2)], axis=1
                    )
                    lanes = pl.ds(half * LANES, LANES)
                    out_ref[0, rows, lanes] = diag_ref[0, rows, lanes] - term


def assemble(core, mine, other, diag_inv):
    pieces = pl.BlockSpec((8, 32, LANES), lambda s, core_ref: (s, 0, 0))
    block = pl.BlockSpec((1, NB, NB), lambda s, core_ref: (s, 0, 0))
    return pl.pallas_call(
        assemble_kernel,
        grid_spec=pltpu.PrefetchScalarGridSpec(
            num_scalar_prefetch=1,
            grid=(SIBS,),
            in_specs=[pieces, pieces, block],
            out_specs=block,
        ),
        out_shape=jax.ShapeDtypeStruct((SIBS, NB, NB), jnp.float32),
        compiler_params=pltpu.CompilerParams(vmem_limit_bytes=4 * 1024 * 1024),
    )(core, mine, other, diag_inv)


def swap_cores(array):
    return lax.ppermute(array, "core", [(0, 1), (1, 0)])


def shards(trailing, panels, diag_inv, ancestors, owner_map):
    row = lax.axis_index(PROW)
    col = lax.axis_index(PCOL)
    core = lax.axis_index("core")
    nblk = owner_map.shape[0]

    factor_t = panels.T
    moved = lax.ppermute(factor_t, PROW + PCOL, column_of_block())
    partner = swap_cores(trailing)

    beside = row + 1 - 2 * core
    half = col // 16
    blocks = jnp.stack(
        [
            col,
            2 * row,
            2 * row + 1,
            2 * beside,
            2 * beside + 1,
            2 * row + half,
            2 * beside + half,
        ]
    )
    number = jnp.sum(
        jnp.where(owner_map[None, :] == blocks[:, None], jnp.arange(nblk)[None, :], 0), axis=1
    )
    named = jnp.any(ancestors[None, :, :] == number[:, None, None], axis=2)
    sibling = jnp.arange(SIBS, dtype=jnp.int32)[None, :]
    first = jnp.min(jnp.where(named, sibling, SIBS), axis=1)
    last = jnp.max(jnp.where(named, sibling, -1), axis=1)
    slots = jnp.stack([first, last], axis=1)
    chosen = (slots[0][:, None] == sibling).reshape(8)
    matched = (slots[1:5].reshape(8)[:, None] == slots[0][None, :]).reshape(16)
    placed = (slots[5:7].reshape(4)[:, None] == sibling).reshape(16)
    masks = jnp.concatenate([chosen, matched, placed]).astype(jnp.float32)
    masks = lax.optimization_barrier(jnp.broadcast_to(masks[:, None], (40, NB)))
    chosen = masks[0:8].reshape(2, SIBS, 1, NB)
    matched = masks[8:24].reshape(4, 2, 2, 1, 1, NB)
    placed = masks[24:40, :LANES].reshape(2, 2, SIBS, 1, LANES)

    parts = moved.reshape(2, 16, 2, NB).transpose(0, 2, 1, 3).reshape(SIBS, 16, NB)
    parts = exchange(parts, ("xl", "ylo"))
    parts = jnp.sum(chosen * parts[None], axis=1)
    parts, own = lax.optimization_barrier((parts, factor_t))
    block = exchange(to_all(parts.reshape(32, NB), CHIPS), CHIP).reshape(CHIPS, 2, 16, NB)
    across = lax.ppermute(own, "yhi", [(0, 1), (1, 0), (2, 3), (3, 2)])
    right = lax.axis_index("yhi") % 2 == 1
    pair = jnp.concatenate([jnp.where(right, across, own), jnp.where(right, own, across)])

    sides = matched[:, :, 0] * block[None, None, :, 0] + matched[:, :, 1] * block[None, None, :, 1]
    sides = sides.reshape(2, 2, NB, NB)
    products = []
    for tile, side in ((trailing, sides[0]), (partner, sides[1])):
        product = lax.dot_general(
            tile.reshape(2, NB, NB),
            side,
            (((2,), (2,)), ((0,), (0,))),
            precision=HIGH,
            preferred_element_type=jnp.float32,
        )
        products.append(product.reshape(NCOL, 16, NB))
    pieces = exchange(jnp.stack(products, axis=1), PCOL)
    pair_beside = swap_cores(pair)
    pieces, pair, pair_beside = lax.optimization_barrier((pieces, pair, pair_beside))
    reduced = jnp.sum(pieces, axis=0)

    result = -(
        placed[:, 0] * reduced[:, None, :, :LANES] + placed[:, 1] * reduced[:, None, :, LANES:]
    )

    upper = result.reshape(2, SIBS, 16, 2, 64).transpose(1, 3, 2, 0, 4)
    upper = upper.reshape(SIBS, 1, 2, 1, 16, LANES)
    upper = jnp.broadcast_to(upper, (SIBS, 2, 2, 2, 16, LANES)).reshape(NCOL, 16, LANES)
    upper = exchange(upper, PCOL).reshape(512, LANES)

    term = jnp.dot(
        pair, upper[:, :64], precision=HIGH, preferred_element_type=jnp.float32
    ) + jnp.dot(
        pair_beside, upper[:, 64:], precision=HIGH, preferred_element_type=jnp.float32
    )
    term = jnp.concatenate([term[:32], term[32:]], axis=1)
    term = jnp.sum(exchange(to_all(term, CHIPS), CHIP), axis=0)
    mine = exchange(to_all(term, NCOL), PCOL)
    got = swap_cores(result[1])
    low = jnp.where(core == 0, result[0], got)
    high = jnp.where(core == 0, got, result[0])
    inv_panel = jnp.stack([low, high], axis=1).transpose(2, 0, 1, 3).reshape(16, SIBS * NB)
    odd = lax.axis_index("ylo") == 1
    keep = jnp.where(odd, upper[:, 32:64], upper[:, :32]).T
    give = jnp.where(odd, upper[:, 96:], upper[:, 64:96]).T
    inv_upper = jnp.where(lax.axis_index("yhi") // 2 == core, keep, swap_cores(give))
    mine, inv_upper, inv_panel = lax.optimization_barrier((mine, inv_upper, inv_panel))
    other = swap_cores(mine)
    inv_diag = assemble(core.reshape(1), mine, other, diag_inv)

    return (inv_panel, inv_upper, inv_diag)


def solution(mesh):
    grid = Mesh(mesh.devices.reshape(2, 2, 2, 2, 4, 4, 2), PROW + PCOL)
    placed = (P(PROW, PCOL), P(PROW, PCOL), P(), P(), P())
    return jax.shard_map(
        shards,
        mesh=grid,
        in_specs=placed,
        out_specs=(P(PROW + PCOL, None), P(PCOL, PROW), P()),
        check_vma=False,
    )
```

profile of v0, /device:TPU:1, one launch (start us, length us, event | category | flops | bytes accessed | tf_op | source)
XLA Modules:
  0.0 153.4 jit_solution(4687812350374455787)
XLA Ops:
  0.6 5.6 %collective-permute-start = (f32[32,512]{1,0:T(8,128)}, f32[32,512]{1,0:T(8,128)S(1)}, u32[]{:S(2)}, u32[]{:S(2)}) collective-permute-start(f32[32,512]{1,0:T(8,128)} %bitcast.100), channel_id=1, source_target_pairs={{0,0},{1,128},{2,256},{3,384},{4,32},{5,160},{6,288},{7,416},{8,1}... | collective-permute-start | bytes 196616 | tf_op jit(solution)/shard_map/ppermute | solution.py:91
  8.7 3.0 %collective-permute-done = f32[32,512]{1,0:T(8,128)S(1)} collective-permute-done((f32[32,512]{1,0:T(8,128)}, f32[32,512]{1,0:T(8,128)S(1)}, u32[]{:S(2)}, u32[]{:S(2)}) %collective-permute-start) | collective-permute-done | bytes 65568 | tf_op jit(solution)/shard_map/ppermute | solution.py:91
  12.4 13.6 %all-to-all-start = ((f32[4,16,256]{2,1,0:T(8,128)}), f32[4,16,256]{2,1,0:T(8,128)S(1)}, u32[]{:S(2)}, u32[]{:S(2)}) async-start(f32[4,16,256]{2,1,0:T(8,128)} %bitcast.11), calls=%async_computation | async-start | bytes 131072 | tf_op jit(solution)/shard_map/all_to_all | solution.py:21
  26.2 3.5 %all-to-all-done = f32[4,16,256]{2,1,0:T(8,128)S(1)} async-done(((f32[4,16,256]{2,1,0:T(8,128)}), f32[4,16,256]{2,1,0:T(8,128)S(1)}, u32[]{:S(2)}, u32[]{:S(2)}) %all-to-all-start) | async-done | bytes 65568 | tf_op jit(solution)/shard_map/all_to_all | solution.py:21
  30.5 3.4 %all-to-all-start.1 = ((f32[8,32,256]{2,1,0:T(8,128)}), f32[8,32,256]{2,1,0:T(8,128)S(1)}, u32[]{:S(2)}, u32[]{:S(2)}) async-start(f32[8,32,256]{2,1,0:T(8,128)} %broadcast_in_dim.79), calls=%async_computation.1 | async-start | bytes 524288 | tf_op jit(solution)/shard_map/all_to_all | solution.py:21
  33.9 3.0 %collective-permute-start.1 = (f32[512,256]{1,0:T(8,128)S(1)}, f32[512,256]{1,0:T(8,128)S(1)}, u32[]{:S(2)}, u32[]{:S(2)}) collective-permute-start(f32[512,256]{1,0:T(8,128)S(1)} %copy-done.1), channel_id=1, source_target_pairs={{0,32},{32,0},{1,33},{33,1},{2,34},{34,2},{3,35},{35,3},{4,36},{36... | collective-permute-start | bytes 1572872 | tf_op jit(solution)/shard_map/ppermute | solution.py:81
  37.0 2.9 %all-to-all-done.1 = f32[8,32,256]{2,1,0:T(8,128)S(1)} async-done(((f32[8,32,256]{2,1,0:T(8,128)}), f32[8,32,256]{2,1,0:T(8,128)S(1)}, u32[]{:S(2)}, u32[]{:S(2)}) %all-to-all-start.1) | async-done | bytes 262176 | tf_op jit(solution)/shard_map/all_to_all | solution.py:21
  41.0 1.1 pad_maximum_fusion
  42.1 12.3 %all-to-all-start.2 = ((f32[32,2,16,256]{3,2,1,0:T(8,128)}), f32[32,2,16,256]{3,2,1,0:T(8,128)S(1)}, u32[]{:S(2)}, u32[]{:S(2)}) async-start(f32[32,2,16,256]{3,2,1,0:T(8,128)} %pad_maximum_fusion), calls=%async_computation.2 | async-start | bytes 2097152 | tf_op jit(solution)/shard_map/all_to_all | solution.py:21
  54.4 4.0 %collective-permute-start.2 = (f32[32,512]{1,0:T(8,128)S(1)}, f32[32,512]{1,0:T(8,128)S(1)}, u32[]{:S(2)}, u32[]{:S(2)}) collective-permute-start(f32[32,512]{1,0:T(8,128)S(1)} %bitcast.101), channel_id=1, source_target_pairs={{0,2},{2,0},{4,6},{6,4},{1,3},{3,1},{5,7},{7,5},{8,10},{10,8},{12,... | collective-permute-start | bytes 196616 | tf_op jit(solution)/shard_map/ppermute | solution.py:129
  58.5 19.5 %collective-permute-done.2 = f32[32,512]{1,0:T(8,128)S(1)} collective-permute-done((f32[32,512]{1,0:T(8,128)S(1)}, f32[32,512]{1,0:T(8,128)S(1)}, u32[]{:S(2)}, u32[]{:S(2)}) %collective-permute-start.2) | collective-permute-done | bytes 65568 | tf_op jit(solution)/shard_map/ppermute | solution.py:129
  78.0 7.6 %collective-permute-start.3 = (f32[64,512]{1,0:T(8,128)S(1)}, f32[64,512]{1,0:T(8,128)S(1)}, u32[]{:S(2)}, u32[]{:S(2)}) collective-permute-start(f32[64,512]{1,0:T(8,128)S(1)} %pad_maximum_fusion.1), channel_id=1, source_target_pairs={{0,32},{32,0},{1,33},{33,1},{2,34},{34,2},{3,35},{35,3},{4,36},{36... | collective-permute-start | bytes 393224 | tf_op jit(solution)/shard_map/ppermute | solution.py:81
  87.1 22.8 %all_to_all.30 = f32[32,16,128]{2,1,0:T(8,128)S(1)} all-to-all(f32[32,16,128]{2,1,0:T(8,128)S(1)} %bitcast.90), channel_id=1, replica_groups=mesh['zlo'=2,'xh'=2,'xl'=2,'core'=2,'zhi'=4,'yhi'=4,'ylo'=2] {'zhi','yhi..., dimensions={0} | all-to-all | bytes 524288 | tf_op jit(solution)/shard_map/all_to_all | solution.py:21
  111.2 4.8 %all-to-all-start.4 = ((f32[8,32,128]{2,1,0:T(8,128)}), f32[8,32,128]{2,1,0:T(8,128)S(1)}, u32[]{:S(2)}, u32[]{:S(2)}) async-start(f32[8,32,128]{2,1,0:T(8,128)} %broadcast_in_dim.81), calls=%async_computation.4 | async-start | bytes 262144 | tf_op jit(solution)/shard_map/all_to_all | solution.py:21
  116.0 5.4 %all-to-all-done.4 = f32[8,32,128]{2,1,0:T(8,128)S(1)} async-done(((f32[8,32,128]{2,1,0:T(8,128)}), f32[8,32,128]{2,1,0:T(8,128)S(1)}, u32[]{:S(2)}, u32[]{:S(2)}) %all-to-all-start.4) | async-done | bytes 131104 | tf_op jit(solution)/shard_map/all_to_all | solution.py:21
  121.4 0.9 broadcast_in_dim.82
  122.3 5.9 %all-to-all-start.5 = ((f32[32,32,128]{2,1,0:T(8,128)}), f32[32,32,128]{2,1,0:T(8,128)S(1)}, u32[]{:S(2)}, u32[]{:S(2)}) async-start(f32[32,32,128]{2,1,0:T(8,128)} %broadcast_in_dim.82), calls=%async_computation.5 | async-start | bytes 1048576 | tf_op jit(solution)/shard_map/all_to_all | solution.py:21
  128.2 4.6 %collective-permute-start.5 = (f32[4,16,128]{2,0,1:T(4,128)S(1)}, f32[4,16,128]{2,0,1:T(4,128)S(1)}, u32[]{:S(2)}, u32[]{:S(2)}) collective-permute-start(f32[4,16,128]{2,0,1:T(4,128)S(1)} %slice_bitcast_fusion.2), channel_id=1, source_target_pairs={{0,32},{32,0},{1,33},{33,1},{2,34},{34,2},{3,35},{35,3},{4,36},{36... | collective-permute-start | bytes 98312 | tf_op jit(solution)/shard_map/ppermute | solution.py:81
  132.8 0.8 collective-permute-done.5
  133.8 2.4 %collective-permute-start.4 = (f32[32,512]{0,1:T(8,128)S(1)}, f32[32,512]{0,1:T(8,128)S(1)}, u32[]{:S(2)}, u32[]{:S(2)}) collective-permute-start(f32[32,512]{0,1:T(8,128)S(1)} %fusion), channel_id=1, source_target_pairs={{0,32},{32,0},{1,33},{33,1},{2,34},{34,2},{3,35},{35,3},{4,36},{36... | collective-permute-start | bytes 196616 | tf_op jit(solution)/shard_map/ppermute | solution.py:81
  137.5 5.7 %all-to-all-done.5.mine_ref = f32[32,32,128]{2,1,0:T(8,128)S(1)} async-done(((f32[32,32,128]{2,1,0:T(8,128)}), f32[32,32,128]{2,1,0:T(8,128)S(1)}, u32[]{:S(2)}, u32[]{:S(2)}) %all-to-all-start.5) | async-done | bytes 524320 | tf_op jit(solution)/shard_map/all_to_all | solution.py:21
  143.2 6.8 %collective-permute-start.6 = (f32[32,32,128]{2,1,0:T(8,128)S(1)}, f32[32,32,128]{2,1,0:T(8,128)S(1)}, u32[]{:S(2)}, u32[]{:S(2)}) collective-permute-start(f32[32,32,128]{2,1,0:T(8,128)S(1)} %all-to-all-done.5.mine_ref), channel_id=1, source_target_pairs={{0,32},{32,0},{1,33},{33,1},{2,34},{34,2},{3,35},{35,3},{4,36},{36... | collective-permute-start | bytes 1572872 | tf_op jit(solution)/shard_map/ppermute | solution.py:81
  150.8 0.8 collective-permute-done.6.other_ref
  151.6 1.8 %shard_map.76 = f32[4,256,256]{2,1,0:T(8,128)} custom-call(s32[1]{0:T(128)} %bitcast.43.core_ref, f32[32,32,128]{2,1,0:T(8,128)S(1)} %all-to-all-done.5.mine_ref, f32[32,32,128]{2,1,0:T(8,128)S(1)} %collective-permute-done.6.other_ref, f32[4,256,256]{2,1,0:T(8,128)S(1)} %copy-done), custom_call_target="tpu_custom_call" | custom-call | tf_op jit(solution)/shard_map/pallas_call | solution.py:67
  (83 shorter events, 10.1 us)
Async XLA Ops:
  0.6 11.1 %collective-permute-start = (f32[32,512]{1,0:T(8,128)}, f32[32,512]{1,0:T(8,128)S(1)}, u32[]{:S(2)}, u32[]{:S(2)}) collective-permute-start(f32[32,512]{1,0:T(8,128)} %bitcast.100), channel_id=1, source_target_pairs={{0,0},{1,128},{2,256},{3,384},{4,32},{5,160},{6,288},{7,416},{8,1}... | collective-permute-start | bytes 196616 | tf_op jit(solution)/shard_map/ppermute | solution.py:91
  6.3 0.7 copy-start.4
  6.3 0.8 copy-start.3
  12.4 17.3 %all-to-all-start = ((f32[4,16,256]{2,1,0:T(8,128)}), f32[4,16,256]{2,1,0:T(8,128)S(1)}, u32[]{:S(2)}, u32[]{:S(2)}) async-start(f32[4,16,256]{2,1,0:T(8,128)} %bitcast.11), calls=%async_computation | async-start | bytes 131072 | tf_op jit(solution)/shard_map/all_to_all | solution.py:21
  26.0 7.9 %copy-start.1 = (f32[512,256]{1,0:T(8,128)S(1)}, f32[512,256]{1,0:T(8,128)}, u32[]{:S(2)}) copy-start(f32[512,256]{1,0:T(8,128)} %param.5) | copy-start | bytes 1572868
  30.5 9.5 %all-to-all-start.1 = ((f32[8,32,256]{2,1,0:T(8,128)}), f32[8,32,256]{2,1,0:T(8,128)S(1)}, u32[]{:S(2)}, u32[]{:S(2)}) async-start(f32[8,32,256]{2,1,0:T(8,128)} %broadcast_in_dim.79), calls=%async_computation.1 | async-start | bytes 524288 | tf_op jit(solution)/shard_map/all_to_all | solution.py:21
  33.9 6.3 %collective-permute-start.1 = (f32[512,256]{1,0:T(8,128)S(1)}, f32[512,256]{1,0:T(8,128)S(1)}, u32[]{:S(2)}, u32[]{:S(2)}) collective-permute-start(f32[512,256]{1,0:T(8,128)S(1)} %copy-done.1), channel_id=1, source_target_pairs={{0,32},{32,0},{1,33},{33,1},{2,34},{34,2},{3,35},{35,3},{4,36},{36... | collective-permute-start | bytes 1572872 | tf_op jit(solution)/shard_map/ppermute | solution.py:81
  42.1 12.3 %copy-start.2 = (f32[512,32]{0,1:T(8,128)S(1)}, f32[512,32]{0,1:T(8,128)}, u32[]{:S(2)}) copy-start(f32[512,32]{0,1:T(8,128)} %param.6) | copy-start | bytes 196612
  42.1 44.5 %all-to-all-start.2 = ((f32[32,2,16,256]{3,2,1,0:T(8,128)}), f32[32,2,16,256]{3,2,1,0:T(8,128)S(1)}, u32[]{:S(2)}, u32[]{:S(2)}) async-start(f32[32,2,16,256]{3,2,1,0:T(8,128)} %pad_maximum_fusion), calls=%async_computation.2 | async-start | bytes 2097152 | tf_op jit(solution)/shard_map/all_to_all | solution.py:21
  54.4 23.6 %collective-permute-start.2 = (f32[32,512]{1,0:T(8,128)S(1)}, f32[32,512]{1,0:T(8,128)S(1)}, u32[]{:S(2)}, u32[]{:S(2)}) collective-permute-start(f32[32,512]{1,0:T(8,128)S(1)} %bitcast.101), channel_id=1, source_target_pairs={{0,2},{2,0},{4,6},{6,4},{1,3},{3,1},{5,7},{7,5},{8,10},{10,8},{12,... | collective-permute-start | bytes 196616 | tf_op jit(solution)/shard_map/ppermute | solution.py:129
  78.0 8.5 %collective-permute-start.3 = (f32[64,512]{1,0:T(8,128)S(1)}, f32[64,512]{1,0:T(8,128)S(1)}, u32[]{:S(2)}, u32[]{:S(2)}) collective-permute-start(f32[64,512]{1,0:T(8,128)S(1)} %pad_maximum_fusion.1), channel_id=1, source_target_pairs={{0,32},{32,0},{1,33},{33,1},{2,34},{34,2},{3,35},{35,3},{4,36},{36... | collective-permute-start | bytes 393224 | tf_op jit(solution)/shard_map/ppermute | solution.py:81
  111.2 10.3 %all-to-all-start.4 = ((f32[8,32,128]{2,1,0:T(8,128)}), f32[8,32,128]{2,1,0:T(8,128)S(1)}, u32[]{:S(2)}, u32[]{:S(2)}) async-start(f32[8,32,128]{2,1,0:T(8,128)} %broadcast_in_dim.81), calls=%async_computation.4 | async-start | bytes 262144 | tf_op jit(solution)/shard_map/all_to_all | solution.py:21
  122.3 20.9 %all-to-all-start.5 = ((f32[32,32,128]{2,1,0:T(8,128)}), f32[32,32,128]{2,1,0:T(8,128)S(1)}, u32[]{:S(2)}, u32[]{:S(2)}) async-start(f32[32,32,128]{2,1,0:T(8,128)} %broadcast_in_dim.82), calls=%async_computation.5 | async-start | bytes 1048576 | tf_op jit(solution)/shard_map/all_to_all | solution.py:21
  128.2 5.4 %collective-permute-start.5 = (f32[4,16,128]{2,0,1:T(4,128)S(1)}, f32[4,16,128]{2,0,1:T(4,128)S(1)}, u32[]{:S(2)}, u32[]{:S(2)}) collective-permute-start(f32[4,16,128]{2,0,1:T(4,128)S(1)} %slice_bitcast_fusion.2), channel_id=1, source_target_pairs={{0,32},{32,0},{1,33},{33,1},{2,34},{34,2},{3,35},{35,3},{4,36},{36... | collective-permute-start | bytes 98312 | tf_op jit(solution)/shard_map/ppermute | solution.py:81
  133.6 18.0 %copy-start = (f32[4,256,256]{2,1,0:T(8,128)S(1)}, f32[4,256,256]{2,1,0:T(8,128)}, u32[]{:S(2)}) copy-start(f32[4,256,256]{2,1,0:T(8,128)} %diag_ref.1) | copy-start | bytes 3145732
  133.8 3.6 %collective-permute-start.4 = (f32[32,512]{0,1:T(8,128)S(1)}, f32[32,512]{0,1:T(8,128)S(1)}, u32[]{:S(2)}, u32[]{:S(2)}) collective-permute-start(f32[32,512]{0,1:T(8,128)S(1)} %fusion), channel_id=1, source_target_pairs={{0,32},{32,0},{1,33},{33,1},{2,34},{34,2},{3,35},{35,3},{4,36},{36... | collective-permute-start | bytes 196616 | tf_op jit(solution)/shard_map/ppermute | solution.py:81
  143.2 8.4 %collective-permute-start.6 = (f32[32,32,128]{2,1,0:T(8,128)S(1)}, f32[32,32,128]{2,1,0:T(8,128)S(1)}, u32[]{:S(2)}, u32[]{:S(2)}) collective-permute-start(f32[32,32,128]{2,1,0:T(8,128)S(1)} %all-to-all-done.5.mine_ref), channel_id=1, source_target_pairs={{0,32},{32,0},{1,33},{33,1},{2,34},{34,2},{3,35},{35,3},{4,36},{36... | collective-permute-start | bytes 1572872 | tf_op jit(solution)/shard_map/ppermute | solution.py:81
where the time goes:
time: 155 us; the launch traced here: 153 us
  starting transfers between devices  74 us (48%)
  waiting for transfers between devices  42.7 us (28%)
  blocking collectives  22.8 us (15%)
  local copies, waits for them, and re-layouts  6.9 us (4%)
  other arithmetic  2.78 us (2%)
  Pallas kernels  1.83 us (1%)
    all_to_all x5, starting transfers between devices, exchange(): return lax.all_to_all(array, axes, 0, 0, tiled=True)  40 us
    ppermute x5, starting transfers between devices, swap_cores(): return lax.ppermute(array, 'core', [(0, 1), (1, 0)])  24.3 us
    all_to_all x1, blocking collectives, exchange(): return lax.all_to_all(array, axes, 0, 0, tiled=True)  22.8 us
    ppermute x1, waiting for transfers between devices, shards(): across = lax.ppermute(own, 'yhi', [(0, 1), (1, 0), (2, 3), (3, 2)])  19.5 us
    all_to_all x5, waiting for transfers between devices, exchange(): return lax.all_to_all(array, axes, 0, 0, tiled=True)  17.6 us
    ppermute x1, starting transfers between devices, shards(): moved = lax.ppermute(factor_t, PROW + PCOL, column_of_block())  5.6 us
    ppermute x1, starting transfers between devices, shards(): across = lax.ppermute(own, 'yhi', [(0, 1), (1, 0), (2, 3), (3, 2)])  4.04 us
  transfers between devices with their start and end apart: 12, of which 10 were waited for; matrix products, arithmetic and copies ran while one was open for 3% of the time, Pallas kernels for 0%

commit v1 on v0

--- a/solution.py
+++ b/solution.py
@@ -112,25 +112,23 @@
     first = jnp.min(jnp.where(named, sibling, SIBS), axis=1)
     last = jnp.max(jnp.where(named, sibling, -1), axis=1)
     slots = jnp.stack([first, last], axis=1)
-    chosen = (slots[0][:, None] == sibling).reshape(8)
-    matched = (slots[1:5].reshape(8)[:, None] == slots[0][None, :]).reshape(16)
+    held = jnp.any(slots[0][:, None] == sibling, axis=0)
+    matched = ((slots[1:5].reshape(8)[:, None] == sibling) & held[None, :]).reshape(32)
     placed = (slots[5:7].reshape(4)[:, None] == sibling).reshape(16)
-    masks = jnp.concatenate([chosen, matched, placed]).astype(jnp.float32)
-    masks = lax.optimization_barrier(jnp.broadcast_to(masks[:, None], (40, NB)))
-    chosen = masks[0:8].reshape(2, SIBS, 1, NB)
-    matched = masks[8:24].reshape(4, 2, 2, 1, 1, NB)
-    placed = masks[24:40, :LANES].reshape(2, 2, SIBS, 1, LANES)
+    masks = jnp.concatenate([matched, placed]).astype(jnp.float32)
+    masks = lax.optimization_barrier(jnp.broadcast_to(masks[:, None], (48, NB)))
+    matched = masks[0:32].reshape(4, 2, SIBS, 1, 1, NB)
+    placed = masks[32:48, :LANES].reshape(2, 2, SIBS, 1, LANES)
 
-    parts = moved.reshape(2, 16, 2, NB).transpose(0, 2, 1, 3).reshape(SIBS, 16, NB)
-    parts = exchange(parts, ("xl", "ylo"))
-    parts = jnp.sum(chosen * parts[None], axis=1)
-    parts, own = lax.optimization_barrier((parts, factor_t))
-    block = exchange(to_all(parts.reshape(32, NB), CHIPS), CHIP).reshape(CHIPS, 2, 16, NB)
+    halves = moved.reshape(32, 2, NB).transpose(1, 0, 2)
+    halves, own = lax.optimization_barrier((halves, factor_t))
+    halves = to_all(halves, CHIPS)
+    block = exchange(halves.reshape(NROW, 32, NB), CHIP + ("ylo",)).reshape(4, SIBS, 32, NB)
     across = lax.ppermute(own, "yhi", [(0, 1), (1, 0), (2, 3), (3, 2)])
     right = lax.axis_index("yhi") % 2 == 1
     pair = jnp.concatenate([jnp.where(right, across, own), jnp.where(right, own, across)])
 
-    sides = matched[:, :, 0] * block[None, None, :, 0] + matched[:, :, 1] * block[None, None, :, 1]
+    sides = sum(matched[:, :, s] * block[None, None, :, s] for s in range(SIBS))
     sides = sides.reshape(2, 2, NB, NB)
     products = []
     for tile, side in ((trailing, sides[0]), (partner, sides[1])):

time: 155 us -> 148 us (0.955)
  starting transfers between devices: 74 us -> 64.4 us
  waiting for transfers between devices: 42.7 us -> 46 us
    all_to_all x5 -> x4, starting transfers between devices: 40 us -> 32.3 us  [exchange(): return lax.all_to_all(array, axes, 0, 0, tiled=True)]
    all_to_all x5 -> x4, waiting for transfers between devices: 17.6 us -> 20.8 us  [exchange(): return lax.all_to_all(array, axes, 0, 0, tiled=True)]
    ppermute x1, waiting for transfers between devices: 19.5 us -> 22.6 us  [shards(): across = lax.ppermute(own, 'yhi', [(0, 1), (1, 0), (2, 3), (3, 2)])]
    ppermute x1, waiting for transfers between devices: 3.04 us -> 0.01 us  [shards(): moved = lax.ppermute(factor_t, PROW + PCOL, column_of_block())]
    ppermute x5, starting transfers between devices: 24.3 us -> 22.5 us  [swap_cores(): return lax.ppermute(array, 'core', [(0, 1), (1, 0)])]
  transfers between devices with their start and end apart: 12 -> 11, of which waited for: 10 -> 8; matrix products, arithmetic and copies ran while one was open for 3% -> 4% of each run, Pallas kernels for 0% -> 0%
where the time goes in v1:
time: 148 us; the launch traced here: 146 us
  starting transfers between devices  64.4 us (44%)
  waiting for transfers between devices  46 us (31%)
  blocking collectives  22 us (15%)
  local copies, waits for them, and re-layouts  6.98 us (5%)
  other arithmetic  2.89 us (2%)
  Pallas kernels  1.83 us (1%)
    all_to_all x4, starting transfers between devices, exchange(): return lax.all_to_all(array, axes, 0, 0, tiled=True)  32.3 us
    ppermute x1, waiting for transfers between devices, shards(): across = lax.ppermute(own, 'yhi', [(0, 1), (1, 0), (2, 3), (3, 2)])  22.6 us
    ppermute x5, starting transfers between devices, swap_cores(): return lax.ppermute(array, 'core', [(0, 1), (1, 0)])  22.5 us
    all_to_all x1, blocking collectives, exchange(): return lax.all_to_all(array, axes, 0, 0, tiled=True)  22 us
    all_to_all x4, waiting for transfers between devices, exchange(): return lax.all_to_all(array, axes, 0, 0, tiled=True)  20.8 us
    ppermute x1, starting transfers between devices, shards(): moved = lax.ppermute(factor_t, PROW + PCOL, column_of_block())  5.6 us
    ppermute x1, starting transfers between devices, shards(): across = lax.ppermute(own, 'yhi', [(0, 1), (1, 0), (2, 3), (3, 2)])  4.04 us
  transfers between devices with their start and end apart: 11, of which 8 were waited for; matrix products, arithmetic and copies ran while one was open for 4% of the time, Pallas kernels for 0%

profile of v1, /device:TPU:1, one launch (start us, length us, event | category | flops | bytes accessed | tf_op | source)
XLA Modules:
  0.0 146.5 jit_solution(5484449420472121307)
XLA Ops:
  0.6 5.6 %collective-permute-start = (f32[32,512]{1,0:T(8,128)}, f32[32,512]{1,0:T(8,128)S(1)}, u32[]{:S(2)}, u32[]{:S(2)}) collective-permute-start(f32[32,512]{1,0:T(8,128)} %bitcast.106), channel_id=1, source_target_pairs={{0,0},{1,128},{2,256},{3,384},{4,32},{5,160},{6,288},{7,416},{8,1}... | collective-permute-start | bytes 196616 | tf_op jit(solution)/shard_map/ppermute | solution.py:91
  6.2 4.6 %collective-permute-start.1 = (f32[512,256]{1,0:T(8,128)}, f32[512,256]{1,0:T(8,128)S(1)}, u32[]{:S(2)}, u32[]{:S(2)}) collective-permute-start(f32[512,256]{1,0:T(8,128)} %param.5), channel_id=1, source_target_pairs={{0,32},{32,0},{1,33},{33,1},{2,34},{34,2},{3,35},{35,3},{4,36},{36... | collective-permute-start | bytes 1572872 | tf_op jit(solution)/shard_map/ppermute | solution.py:81
  13.2 0.8 broadcast_in_dim.77
  14.0 14.4 %all-to-all-start = ((f32[16,32,256]{2,1,0:T(8,128)}), f32[16,32,256]{2,1,0:T(8,128)S(1)}, u32[]{:S(2)}, u32[]{:S(2)}) async-start(f32[16,32,256]{2,1,0:T(8,128)} %bitcast.11), calls=%async_computation | async-start | bytes 1048576 | tf_op jit(solution)/shard_map/all_to_all | solution.py:21
  28.8 9.4 %all-to-all-done = f32[16,32,256]{2,1,0:T(8,128)S(1)} async-done(((f32[16,32,256]{2,1,0:T(8,128)}), f32[16,32,256]{2,1,0:T(8,128)S(1)}, u32[]{:S(2)}, u32[]{:S(2)}) %all-to-all-start) | async-done | bytes 524320 | tf_op jit(solution)/shard_map/all_to_all | solution.py:21
  40.1 1.1 pad_maximum_fusion
  41.1 8.4 %all-to-all-start.1 = ((f32[32,2,16,256]{3,2,1,0:T(8,128)}), f32[32,2,16,256]{3,2,1,0:T(8,128)S(1)}, u32[]{:S(2)}, u32[]{:S(2)}) async-start(f32[32,2,16,256]{3,2,1,0:T(8,128)} %pad_maximum_fusion), calls=%async_computation.1 | async-start | bytes 2097152 | tf_op jit(solution)/shard_map/all_to_all | solution.py:21
  49.6 4.0 %collective-permute-start.2 = (f32[32,512]{1,0:T(8,128)S(1)}, f32[32,512]{1,0:T(8,128)S(1)}, u32[]{:S(2)}, u32[]{:S(2)}) collective-permute-start(f32[32,512]{1,0:T(8,128)S(1)} %bitcast.107), channel_id=1, source_target_pairs={{0,2},{2,0},{4,6},{6,4},{1,3},{3,1},{5,7},{7,5},{8,10},{10,8},{12,... | collective-permute-start | bytes 196616 | tf_op jit(solution)/shard_map/ppermute | solution.py:127
  53.6 22.6 %collective-permute-done.2 = f32[32,512]{1,0:T(8,128)S(1)} collective-permute-done((f32[32,512]{1,0:T(8,128)S(1)}, f32[32,512]{1,0:T(8,128)S(1)}, u32[]{:S(2)}, u32[]{:S(2)}) %collective-permute-start.2) | collective-permute-done | bytes 65568 | tf_op jit(solution)/shard_map/ppermute | solution.py:127
  76.3 4.5 %collective-permute-start.3 = (f32[64,512]{1,0:T(8,128)S(1)}, f32[64,512]{1,0:T(8,128)S(1)}, u32[]{:S(2)}, u32[]{:S(2)}) collective-permute-start(f32[64,512]{1,0:T(8,128)S(1)} %pad_maximum_fusion.1), channel_id=1, source_target_pairs={{0,32},{32,0},{1,33},{33,1},{2,34},{34,2},{3,35},{35,3},{4,36},{36... | collective-permute-start | bytes 393224 | tf_op jit(solution)/shard_map/ppermute | solution.py:81
  82.3 22.0 %all_to_all.25 = f32[32,16,128]{2,1,0:T(8,128)S(1)} all-to-all(f32[32,16,128]{2,1,0:T(8,128)S(1)} %bitcast.98), channel_id=1, replica_groups=mesh['zlo'=2,'xh'=2,'xl'=2,'core'=2,'zhi'=4,'yhi'=4,'ylo'=2] {'zhi','yhi..., dimensions={0} | all-to-all | bytes 524288 | tf_op jit(solution)/shard_map/all_to_all | solution.py:21
  105.5 3.4 %all-to-all-start.3 = ((f32[8,32,128]{2,1,0:T(8,128)}), f32[8,32,128]{2,1,0:T(8,128)S(1)}, u32[]{:S(2)}, u32[]{:S(2)}) async-start(f32[8,32,128]{2,1,0:T(8,128)} %broadcast_in_dim.79), calls=%async_computation.3 | async-start | bytes 262144 | tf_op jit(solution)/shard_map/all_to_all | solution.py:21
  108.9 5.3 %all-to-all-done.3 = f32[8,32,128]{2,1,0:T(8,128)S(1)} async-done(((f32[8,32,128]{2,1,0:T(8,128)}), f32[8,32,128]{2,1,0:T(8,128)S(1)}, u32[]{:S(2)}, u32[]{:S(2)}) %all-to-all-start.3) | async-done | bytes 131104 | tf_op jit(solution)/shard_map/all_to_all | solution.py:21
  114.3 0.9 broadcast_in_dim.80
  115.1 6.1 %all-to-all-start.4 = ((f32[32,32,128]{2,1,0:T(8,128)}), f32[32,32,128]{2,1,0:T(8,128)S(1)}, u32[]{:S(2)}, u32[]{:S(2)}) async-start(f32[32,32,128]{2,1,0:T(8,128)} %broadcast_in_dim.80), calls=%async_computation.4 | async-start | bytes 1048576 | tf_op jit(solution)/shard_map/all_to_all | solution.py:21
  121.3 4.3 %collective-permute-start.5 = (f32[4,16,128]{2,0,1:T(4,128)S(1)}, f32[4,16,128]{2,0,1:T(4,128)S(1)}, u32[]{:S(2)}, u32[]{:S(2)}) collective-permute-start(f32[4,16,128]{2,0,1:T(4,128)S(1)} %slice_bitcast_fusion.4), channel_id=1, source_target_pairs={{0,32},{32,0},{1,33},{33,1},{2,34},{34,2},{3,35},{35,3},{4,36},{36... | collective-permute-start | bytes 98312 | tf_op jit(solution)/shard_map/ppermute | solution.py:81
  125.7 0.8 collective-permute-done.5
  126.7 2.4 %collective-permute-start.4 = (f32[32,512]{0,1:T(8,128)S(1)}, f32[32,512]{0,1:T(8,128)S(1)}, u32[]{:S(2)}, u32[]{:S(2)}) collective-permute-start(f32[32,512]{0,1:T(8,128)S(1)} %fusion), channel_id=1, source_target_pairs={{0,32},{32,0},{1,33},{33,1},{2,34},{34,2},{3,35},{35,3},{4,36},{36... | collective-permute-start | bytes 196616 | tf_op jit(solution)/shard_map/ppermute | solution.py:81
  129.2 0.7 reshape.122
  130.4 6.1 %all-to-all-done.4.mine_ref = f32[32,32,128]{2,1,0:T(8,128)S(1)} async-done(((f32[32,32,128]{2,1,0:T(8,128)}), f32[32,32,128]{2,1,0:T(8,128)S(1)}, u32[]{:S(2)}, u32[]{:S(2)}) %all-to-all-start.4) | async-done | bytes 524320 | tf_op jit(solution)/shard_map/all_to_all | solution.py:21
  136.5 6.6 %collective-permute-start.6 = (f32[32,32,128]{2,1,0:T(8,128)S(1)}, f32[32,32,128]{2,1,0:T(8,128)S(1)}, u32[]{:S(2)}, u32[]{:S(2)}) collective-permute-start(f32[32,32,128]{2,1,0:T(8,128)S(1)} %all-to-all-done.4.mine_ref), channel_id=1, source_target_pairs={{0,32},{32,0},{1,33},{33,1},{2,34},{34,2},{3,35},{35,3},{4,36},{36... | collective-permute-start | bytes 1572872 | tf_op jit(solution)/shard_map/ppermute | solution.py:81
  143.1 0.7 copy.51
  143.9 0.8 collective-permute-done.6.other_ref
  144.6 1.8 %shard_map.76 = f32[4,256,256]{2,1,0:T(8,128)} custom-call(s32[1]{0:T(128)} %bitcast.44.core_ref, f32[32,32,128]{2,1,0:T(8,128)S(1)} %all-to-all-done.4.mine_ref, f32[32,32,128]{2,1,0:T(8,128)S(1)} %collective-permute-done.6.other_ref, f32[4,256,256]{2,1,0:T(8,128)S(1)} %copy-done), custom_call_target="tpu_custom_call" | custom-call | tf_op jit(solution)/shard_map/pallas_call | solution.py:67
  (78 shorter events, 8.0 us)
Async XLA Ops:
  0.6 12.5 %collective-permute-start = (f32[32,512]{1,0:T(8,128)}, f32[32,512]{1,0:T(8,128)S(1)}, u32[]{:S(2)}, u32[]{:S(2)}) collective-permute-start(f32[32,512]{1,0:T(8,128)} %bitcast.106), channel_id=1, source_target_pairs={{0,0},{1,128},{2,256},{3,384},{4,32},{5,160},{6,288},{7,416},{8,1}... | collective-permute-start | bytes 196616 | tf_op jit(solution)/shard_map/ppermute | solution.py:91
  6.2 32.4 %collective-permute-start.1 = (f32[512,256]{1,0:T(8,128)}, f32[512,256]{1,0:T(8,128)S(1)}, u32[]{:S(2)}, u32[]{:S(2)}) collective-permute-start(f32[512,256]{1,0:T(8,128)} %param.5), channel_id=1, source_target_pairs={{0,32},{32,0},{1,33},{33,1},{2,34},{34,2},{3,35},{35,3},{4,36},{36... | collective-permute-start | bytes 1572872 | tf_op jit(solution)/shard_map/ppermute | solution.py:81
  10.9 0.7 copy-start.4
  10.9 0.8 copy-start.3
  14.0 24.2 %all-to-all-start = ((f32[16,32,256]{2,1,0:T(8,128)}), f32[16,32,256]{2,1,0:T(8,128)S(1)}, u32[]{:S(2)}, u32[]{:S(2)}) async-start(f32[16,32,256]{2,1,0:T(8,128)} %bitcast.11), calls=%async_computation | async-start | bytes 1048576 | tf_op jit(solution)/shard_map/all_to_all | solution.py:21
  38.6 1.0 copy-start.1
  41.1 8.4 %copy-start.2 = (f32[512,32]{0,1:T(8,128)S(1)}, f32[512,32]{0,1:T(8,128)}, u32[]{:S(2)}) copy-start(f32[512,32]{0,1:T(8,128)} %param.6) | copy-start | bytes 196612
  41.1 40.6 %all-to-all-start.1 = ((f32[32,2,16,256]{3,2,1,0:T(8,128)}), f32[32,2,16,256]{3,2,1,0:T(8,128)S(1)}, u32[]{:S(2)}, u32[]{:S(2)}) async-start(f32[32,2,16,256]{3,2,1,0:T(8,128)} %pad_maximum_fusion), calls=%async_computation.1 | async-start | bytes 2097152 | tf_op jit(solution)/shard_map/all_to_all | solution.py:21
  49.6 26.6 %collective-permute-start.2 = (f32[32,512]{1,0:T(8,128)S(1)}, f32[32,512]{1,0:T(8,128)S(1)}, u32[]{:S(2)}, u32[]{:S(2)}) collective-permute-start(f32[32,512]{1,0:T(8,128)S(1)} %bitcast.107), channel_id=1, source_target_pairs={{0,2},{2,0},{4,6},{6,4},{1,3},{3,1},{5,7},{7,5},{8,10},{10,8},{12,... | collective-permute-start | bytes 196616 | tf_op jit(solution)/shard_map/ppermute | solution.py:127
  76.3 5.5 %collective-permute-start.3 = (f32[64,512]{1,0:T(8,128)S(1)}, f32[64,512]{1,0:T(8,128)S(1)}, u32[]{:S(2)}, u32[]{:S(2)}) collective-permute-start(f32[64,512]{1,0:T(8,128)S(1)} %pad_maximum_fusion.1), channel_id=1, source_target_pairs={{0,32},{32,0},{1,33},{33,1},{2,34},{34,2},{3,35},{35,3},{4,36},{36... | collective-permute-start | bytes 393224 | tf_op jit(solution)/shard_map/ppermute | solution.py:81
  105.5 8.7 %all-to-all-start.3 = ((f32[8,32,128]{2,1,0:T(8,128)}), f32[8,32,128]{2,1,0:T(8,128)S(1)}, u32[]{:S(2)}, u32[]{:S(2)}) async-start(f32[8,32,128]{2,1,0:T(8,128)} %broadcast_in_dim.79), calls=%async_computation.3 | async-start | bytes 262144 | tf_op jit(solution)/shard_map/all_to_all | solution.py:21
  115.1 21.3 %all-to-all-start.4 = ((f32[32,32,128]{2,1,0:T(8,128)}), f32[32,32,128]{2,1,0:T(8,128)S(1)}, u32[]{:S(2)}, u32[]{:S(2)}) async-start(f32[32,32,128]{2,1,0:T(8,128)} %broadcast_in_dim.80), calls=%async_computation.4 | async-start | bytes 1048576 | tf_op jit(solution)/shard_map/all_to_all | solution.py:21
  121.3 5.2 %collective-permute-start.5 = (f32[4,16,128]{2,0,1:T(4,128)S(1)}, f32[4,16,128]{2,0,1:T(4,128)S(1)}, u32[]{:S(2)}, u32[]{:S(2)}) collective-permute-start(f32[4,16,128]{2,0,1:T(4,128)S(1)} %slice_bitcast_fusion.4), channel_id=1, source_target_pairs={{0,32},{32,0},{1,33},{33,1},{2,34},{34,2},{3,35},{35,3},{4,36},{36... | collective-permute-start | bytes 98312 | tf_op jit(solution)/shard_map/ppermute | solution.py:81
  126.5 18.2 %copy-start = (f32[4,256,256]{2,1,0:T(8,128)S(1)}, f32[4,256,256]{2,1,0:T(8,128)}, u32[]{:S(2)}) copy-start(f32[4,256,256]{2,1,0:T(8,128)} %diag_ref.1) | copy-start | bytes 3145732
  126.7 3.6 %collective-permute-start.4 = (f32[32,512]{0,1:T(8,128)S(1)}, f32[32,512]{0,1:T(8,128)S(1)}, u32[]{:S(2)}, u32[]{:S(2)}) collective-permute-start(f32[32,512]{0,1:T(8,128)S(1)} %fusion), channel_id=1, source_target_pairs={{0,32},{32,0},{1,33},{33,1},{2,34},{34,2},{3,35},{35,3},{4,36},{36... | collective-permute-start | bytes 196616 | tf_op jit(solution)/shard_map/ppermute | solution.py:81
  136.5 8.2 %collective-permute-start.6 = (f32[32,32,128]{2,1,0:T(8,128)S(1)}, f32[32,32,128]{2,1,0:T(8,128)S(1)}, u32[]{:S(2)}, u32[]{:S(2)}) collective-permute-start(f32[32,32,128]{2,1,0:T(8,128)S(1)} %all-to-all-done.4.mine_ref), channel_id=1, source_target_pairs={{0,32},{32,0},{1,33},{33,1},{2,34},{34,2},{3,35},{35,3},{4,36},{36... | collective-permute-start | bytes 1572872 | tf_op jit(solution)/shard_map/ppermute | solution.py:81
